TPU v7x, 32 devices: a whole 2x2x4 slice. The times are simulated.
32 devices in a mesh: loop: 4 (over y, core), inner: 8 (over z, x).
Axes of the slice: x: 2, y: 2, z: 4, core: 2. Of those that a mesh axis runs over, the one named last changes fastest.
Arguments:
- snapshots: bfloat16 [8192, 1024], P(('loop', 'inner')), may hold values from -6 to 6
- bins: int32 [8192], replicated, may hold values from 0 to 63, as said below
- pairs: int32 [256, 2], replicated, may hold values from 0 to 63, as said below
- start_weights: bfloat16 [1024, 32], replicated, may hold values from -0.1875 to 0.1875
Outputs:
- basis: float32 [8192, 96], P(('loop', 'inner'))
- coefficients: float32 [4, 32, 32], replicated
Inputs may be any that keep to these rules, and one draw needn't show every extreme that they name: `bins`: the snapshot in row n has a bin in [r * 8, (r + 1) * 8), where r = (n // 256) mod (8). `pairs`: every row (a, b) has a <= b <= a + 8; every bin is paired with itself.
All inputs are finite; a program needn't handle non-finite values.
Results may differ from a plain program's by a relative error of at most 0.0003.
Values may be sent and summed in bfloat16 or wider, within the bound.
No kernel may reach another device: no remote copies, remote signals or barrier semaphores. Data moves between devices by JAX's collectives and lax.ppermute only.
A program may use at most 64 MiB of HBM per device.

v0:
```python
import jax
import jax.numpy as jnp
from jax import lax
from jax.sharding import PartitionSpec as P

STEPS = 2
BINS_COL = 8


def extended(cells, sides, width):
    for axis, dim in sides:
        count = lax.axis_size(axis)
        ends = count - 1
        head = lax.slice_in_dim(cells, 0, width, axis=dim)
        tail = lax.slice_in_dim(cells, cells.shape[dim] - width, cells.shape[dim], axis=dim)
        cells = jnp.concatenate(
            [
                lax.ppermute(tail, axis, [(i, (i + 1) % count) for i in range(ends)]),
                cells,
                lax.ppermute(head, axis, [((i + 1) % count, i) for i in range(ends)]),
            ],
            axis=dim,
        )
    return cells


def matches(values, targets):
    return (values[:, None] == targets[None, :]).astype(jnp.float32)


def local_gram(left, right):
    return jnp.dot(left.T, right, precision=lax.Precision.HIGHEST)


def finish(matrix, gram_total):
    lower_factor = jnp.linalg.cholesky(gram_total)
    result = lax.linalg.triangular_solve(
        lower_factor, matrix, left_side=False, lower=True, transpose_a=True
    )
    return (result, lower_factor.T)


def local(snapshots, bins, pairs, start_weights):
    row_count, features = snapshots.shape
    block_width = start_weights.shape[1]
    n_loop = lax.axis_size("loop")
    n_inner = lax.axis_size("inner")
    column = lax.axis_index("inner")
    group = lax.axis_index("loop")
    bin_grid = jnp.pad(
        bins.reshape(n_loop, n_inner, row_count), ((0, 0), (1, 1), (0, 0)), constant_values=-1
    )
    side_rows = extended(snapshots, (("inner", 0),), row_count)
    partner_rows = lax.all_gather(side_rows[None], "loop", axis=0, tiled=True)
    tile_rows = partner_rows.reshape(n_loop * 3 * row_count, features)
    tile_bins = lax.dynamic_slice_in_dim(bin_grid, column, 3, 1).reshape(-1)
    my_bins = lax.dynamic_slice_in_dim(bins, (group * n_inner + column) * row_count, row_count)
    bin_base = column * BINS_COL
    my_ids = bin_base + jnp.arange(BINS_COL, dtype=jnp.int32)
    window_ids = bin_base - BINS_COL + jnp.arange(3 * BINS_COL, dtype=jnp.int32)
    left_bins = pairs[:, 0]
    right_bins = pairs[:, 1]
    pair_count = jnp.dot(
        matches(left_bins, my_ids).T,
        matches(right_bins, window_ids),
        precision=lax.Precision.HIGHEST,
    )
    pair_count = pair_count + jnp.dot(
        matches(right_bins, my_ids).T,
        matches(left_bins, window_ids),
        precision=lax.Precision.HIGHEST,
    )
    linked_bins = jnp.where(pair_count > 0.5, 1.0, 0.0).astype(jnp.float32)
    my_hot = matches(my_bins, my_ids)
    row_links = jnp.dot(my_hot, linked_bins)
    mine_wide = snapshots.astype(jnp.float32)
    mine_norms = jnp.sum(mine_wide * mine_wide, axis=1)
    epsilon = features / 3.0
    part_hot = matches(tile_bins, window_ids) * (tile_bins >= 0).astype(jnp.float32)[:, None]
    band_mask = jnp.dot(row_links, part_hot.T)
    part_wide = tile_rows.astype(jnp.float32)
    part_norms = jnp.sum(part_wide * part_wide, axis=1)
    products = lax.dot_general(
        snapshots, tile_rows, (((1,), (1,)), ((), ())), preferred_element_type=jnp.float32
    )
    distance = mine_norms[:, None] + part_norms[None, :] - 2.0 * products
    kept_tiles = [band_mask * jnp.exp(-distance / epsilon)]

    def current_kernel(which):
        return kept_tiles[which]

    degree = jnp.sum(current_kernel(0), axis=1)
    inv_root = lax.rsqrt(degree)
    start_block = jnp.dot(snapshots, start_weights, preferred_element_type=jnp.float32)
    start_total = lax.psum(local_gram(start_block, start_block), ("loop", "inner"))
    current, unused = finish(start_block, start_total)
    basis_blocks = [current]
    coefficients = []
    previous = current
    prev_b = jnp.zeros((block_width, block_width), jnp.float32)
    for lanczos_step in range(STEPS):
        scaled = inv_root[:, None] * current
        vec_side = extended(scaled, (("inner", 0),), row_count)
        vec_strip = lax.all_gather(vec_side[None], "loop", axis=0, tiled=True)
        strip = vec_strip.reshape(n_loop * 3 * row_count, block_width)
        total = jnp.dot(current_kernel(0), strip, precision=lax.Precision.HIGHEST)
        image = inv_root[:, None] * total
        projected = lax.psum(local_gram(current, image), ("loop", "inner"))
        image = image - jnp.dot(current, projected, precision=lax.Precision.HIGHEST)
        if lanczos_step > 0:
            image = image - jnp.dot(previous, prev_b.T, precision=lax.Precision.HIGHEST)
        gram_total = lax.psum(local_gram(image, image), ("loop", "inner"))
        following, factor = finish(image, gram_total)
        coefficients.append(projected)
        coefficients.append(factor)
        previous = current
        prev_b = factor
        current = following
        basis_blocks.append(current)
    return (jnp.concatenate(basis_blocks, axis=1), jnp.stack(coefficients))


def solution(mesh):
    in_specs = (P(("loop", "inner"), None), P(), P(), P())
    out_specs = (P(("loop", "inner"), None), P())
    return jax.shard_map(local, mesh=mesh, in_specs=in_specs, out_specs=out_specs, check_vma=False)
```

profile of v0, /device:TPU:0, one launch (start us, length us, event | category | flops | bytes accessed | tf_op | source)
XLA Modules:
  0.0 321.3 jit_solution(17234646396150438926)
XLA Ops:
  7.3 1.4 collective-permute-start.1
  8.7 5.5 %collective-permute-start = (bf16[256,1024]{1,0:T(8,128)(2,1)}, bf16[256,1024]{1,0:T(8,128)(2,1)S(1)}, u32[]{:S(2)}, u32[]{:S(2)}) collective-permute-start(bf16[256,1024]{1,0:T(8,128)(2,1)} %param.7), channel_id=1, source_target_pairs={{0,1},{1,2},{2,3},{3,4},{4,5},{5,6},{6,7},{8,9},{9,10},{10,11},{11... | collective-permute-start | bytes 1572872 | tf_op jit(solution)/shard_map/ppermute | solution.py:18
  14.2 10.2 %collective-permute-done.1 = bf16[256,1024]{1,0:T(8,128)(2,1)S(1)} collective-permute-done((bf16[256,1024]{1,0:T(8,128)(2,1)}, bf16[256,1024]{1,0:T(8,128)(2,1)S(1)}, u32[]{:S(2)}, u32[]{:S(2)}) %collective-permute-start.1) | collective-permute-done | bytes 524320 | tf_op jit(solution)/shard_map/ppermute | solution.py:20
  24.4 11.5 %collective-permute-done = bf16[256,1024]{1,0:T(8,128)(2,1)S(1)} collective-permute-done((bf16[256,1024]{1,0:T(8,128)(2,1)}, bf16[256,1024]{1,0:T(8,128)(2,1)S(1)}, u32[]{:S(2)}, u32[]{:S(2)}) %collective-permute-start) | collective-permute-done | bytes 524320 | tf_op jit(solution)/shard_map/ppermute | solution.py:18
  35.9 2.3 pad_maximum_fusion
  38.4 0.2 fusion.55
  38.6 0.2 fusion.56
  38.8 42.3 %psum.35 = f32[32,32]{0,1:T(8,128)S(1)} all-reduce(f32[32,32]{0,1:T(8,128)S(1)} %fusion.56), channel_id=1, replica_groups=mesh['loop'=4,'inner'=8] {'loop','inner'}, use_global_device_ids=true, to_apply=%region_0.1 | all-reduce | flops 1024 | bytes 8192 | tf_op jit(solution)/shard_map/psum | solution.py:95
  81.2 2.9 cholesky.59
  84.1 0.6 compare_reduce_fusion.2
  84.8 0.7 fusion.35
  85.4 2.4 custom-call.7
  87.9 0.2 multiply_reduce_fusion.1
  88.1 0.3 fusion.20
  88.4 0.3 fusion.9
  88.7 4.2 %multiply_reduce_fusion = f32[3072]{0:T(1024)S(1)} fusion(bf16[3072,1024]{1,0:T(8,128)(2,1)} %all-gather.5.cloned.1.call-done), kind=kLoop, calls=%fused_computation | loop fusion | flops 9434112 | bytes 6303744 | tf_op jit(solution)/shard_map/reduce_sum | solution.py:82
  92.9 0.4 copy-done.1
  93.3 4.0 %fusion.4 = f32[256,3072]{1,0:T(8,128)} fusion(bf16[3072,1024]{1,0:T(8,128)(2,1)S(1)} %copy-done.1, bf16[256,1024]{1,0:T(8,128)(2,1)S(1)} %copy-done.2, f32[3072]{0:T(1024)S(1)} %multiply_reduce_fusion, f32[256]{0:T(256)S(1)} %multiply_reduce_fusion.1), kind=kOutput, calls=%fused_computation.7 | convolution fusion | flops 1614544896 | bytes 9974784 | tf_op jit(solution)/shard_map/dot_general | solution.py:83
  97.3 2.8 fusion.52
  100.1 0.2 broadcast_multiply_fusion.1
  100.3 1.3 collective-permute-start.3
  101.6 4.8 %collective-permute-start.2 = (f32[256,32]{0,1:T(8,128)S(1)}, f32[256,32]{0,1:T(8,128)S(1)}, u32[]{:S(2)}, u32[]{:S(2)}) collective-permute-start(f32[256,32]{0,1:T(8,128)S(1)} %get-tuple-element.18), channel_id=1, source_target_pairs={{0,1},{1,2},{2,3},{3,4},{4,5},{5,6},{6,7},{8,9},{9,10},{10,11},{11... | collective-permute-start | bytes 98312 | tf_op jit(solution)/shard_map/ppermute | solution.py:18
  106.4 1.6 collective-permute-done.2
  108.0 7.2 %all-gather.1 = f32[3072,32]{0,1:T(8,128)S(1)} all-gather(f32[768,32]{0,1:T(8,128)S(1)} %pad_maximum_fusion.1), channel_id=3, replica_groups=mesh['loop'=4,'inner'=8] {'loop'}, dimensions={0}, use_global_device_ids=true | all-gather | bytes 491520 | tf_op jit(solution)/shard_map/all_gather | solution.py:104
  115.2 2.8 convolution_multiply_fusion.3
  118.1 41.4 %psum.36 = f32[32,32]{0,1:T(8,128)S(1)} all-reduce(f32[32,32]{0,1:T(8,128)S(1)} %fusion.57), channel_id=1, replica_groups=mesh['loop'=4,'inner'=8] {'loop','inner'}, use_global_device_ids=true, to_apply=%region_6.9 | all-reduce | flops 1024 | bytes 8192 | tf_op jit(solution)/shard_map/psum | solution.py:108
  159.7 0.2 fusion.58
  159.9 39.5 %psum.37 = f32[32,32]{0,1:T(8,128)S(1)} all-reduce(f32[32,32]{0,1:T(8,128)S(1)} %fusion.58), channel_id=1, replica_groups=mesh['loop'=4,'inner'=8] {'loop','inner'}, use_global_device_ids=true, to_apply=%region_7.10 | all-reduce | flops 1024 | bytes 8192 | tf_op jit(solution)/shard_map/psum | solution.py:112
  199.4 2.9 cholesky.70
  202.4 0.6 compare_reduce_fusion.1
  203.0 0.7 fusion.43
  203.7 2.4 custom-call.8
  206.1 0.2 broadcast_multiply_fusion
  206.4 1.3 collective-permute-start.5
  207.7 4.8 %collective-permute-start.4 = (f32[256,32]{0,1:T(8,128)S(1)}, f32[256,32]{0,1:T(8,128)S(1)}, u32[]{:S(2)}, u32[]{:S(2)}) collective-permute-start(f32[256,32]{0,1:T(8,128)S(1)} %get-tuple-element.20), channel_id=1, source_target_pairs={{0,1},{1,2},{2,3},{3,4},{4,5},{5,6},{6,7},{8,9},{9,10},{10,11},{11... | collective-permute-start | bytes 98312 | tf_op jit(solution)/shard_map/ppermute | solution.py:18
  212.5 0.9 fusion.44
  213.4 0.7 collective-permute-done.4
  214.1 7.2 %all-gather.2 = f32[3072,32]{0,1:T(8,128)S(1)} all-gather(f32[768,32]{0,1:T(8,128)S(1)} %pad_maximum_fusion.2), channel_id=4, replica_groups=mesh['loop'=4,'inner'=8] {'loop'}, dimensions={0}, use_global_device_ids=true | all-gather | bytes 491520 | tf_op jit(solution)/shard_map/all_gather | solution.py:104
  221.3 2.8 convolution_multiply_fusion.2
  224.2 41.7 %psum.38 = f32[32,32]{0,1:T(8,128)S(1)} all-reduce(f32[32,32]{0,1:T(8,128)S(1)} %fusion.59), channel_id=1, replica_groups=mesh['loop'=4,'inner'=8] {'loop','inner'}, use_global_device_ids=true, to_apply=%region_8.11 | all-reduce | flops 1024 | bytes 8192 | tf_op jit(solution)/shard_map/psum | solution.py:108
  266.3 39.8 %psum.39 = f32[32,32]{0,1:T(8,128)S(1)} all-reduce(f32[32,32]{0,1:T(8,128)S(1)} %fusion.60), channel_id=1, replica_groups=mesh['loop'=4,'inner'=8] {'loop','inner'}, use_global_device_ids=true, to_apply=%region_9.12 | all-reduce | flops 1024 | bytes 8192 | tf_op jit(solution)/shard_map/psum | solution.py:112
  306.2 2.9 cholesky.81
  309.1 0.6 compare_reduce_fusion
  309.8 0.7 fusion.42
  310.4 2.4 custom-call.9
  312.9 0.2 convolution_bitcast_fusion
  313.1 0.6 pad_maximum_fusion.3
  313.8 0.7 copy.35
  (40 shorter events, 1.4 us)
Async XLA Ops:
  7.2 31.2 %copy-start = (bf16[1024,32]{0,1:T(8,128)(2,1)S(1)}, bf16[1024,32]{0,1:T(8,128)(2,1)}, u32[]{:S(2)}) copy-start(bf16[1024,32]{0,1:T(8,128)(2,1)} %param.10) | copy-start | bytes 196612
  7.2 31.2 %copy-start.2 = (bf16[256,1024]{1,0:T(8,128)(2,1)S(1)}, bf16[256,1024]{1,0:T(8,128)(2,1)}, u32[]{:S(2)}) copy-start(bf16[256,1024]{1,0:T(8,128)(2,1)} %param.7) | copy-start | bytes 1572868
  7.2 31.0 %copy-start.3 = (s32[8192]{0:T(1024)S(1)}, s32[8192]{0:T(1024)}, u32[]{:S(2)}) copy-start(s32[8192]{0:T(1024)} %param.8) | copy-start | bytes 98308
  7.2 80.9 %copy-start.4 = (s32[256,2]{0,1:T(2,128)S(1)}, s32[256,2]{0,1:T(2,128)}, u32[]{:S(2)}) copy-start(s32[256,2]{0,1:T(2,128)} %param.9) | copy-start | bytes 6148
  7.2 81.4 %all-gather.5.cloned.1.call-start = ((), (), s32[]{:S(2)}) async-start(), calls=%async_computation | async-start | bytes 7864320 | tf_op jit(solution)/shard_map/all_gather | solution.py:54
  7.3 17.1 %collective-permute-start.1 = (bf16[256,1024]{1,0:T(8,128)(2,1)}, bf16[256,1024]{1,0:T(8,128)(2,1)S(1)}, u32[]{:S(2)}, u32[]{:S(2)}) collective-permute-start(bf16[256,1024]{1,0:T(8,128)(2,1)} %param.7), channel_id=1, source_target_pairs={{1,0},{2,1},{3,2},{4,3},{5,4},{6,5},{7,6},{9,8},{10,9},{11,10},{12... | collective-permute-start | bytes 1572872 | tf_op jit(solution)/shard_map/ppermute | solution.py:20
  8.7 27.2 %collective-permute-start = (bf16[256,1024]{1,0:T(8,128)(2,1)}, bf16[256,1024]{1,0:T(8,128)(2,1)S(1)}, u32[]{:S(2)}, u32[]{:S(2)}) collective-permute-start(bf16[256,1024]{1,0:T(8,128)(2,1)} %param.7), channel_id=1, source_target_pairs={{0,1},{1,2},{2,3},{3,4},{4,5},{5,6},{6,7},{8,9},{9,10},{10,11},{11... | collective-permute-start | bytes 1572872 | tf_op jit(solution)/shard_map/ppermute | solution.py:18
  88.7 4.6 %copy-start.1 = (bf16[3072,1024]{1,0:T(8,128)(2,1)S(1)}, bf16[3072,1024]{1,0:T(8,128)(2,1)}, u32[]{:S(2)}) copy-start(bf16[3072,1024]{1,0:T(8,128)(2,1)} %all-gather.5.cloned.1.call-done) | copy-start | bytes 18874372
  100.3 6.1 %collective-permute-start.3 = (f32[256,32]{0,1:T(8,128)S(1)}, f32[256,32]{0,1:T(8,128)S(1)}, u32[]{:S(2)}, u32[]{:S(2)}) collective-permute-start(f32[256,32]{0,1:T(8,128)S(1)} %get-tuple-element.18), channel_id=1, source_target_pairs={{1,0},{2,1},{3,2},{4,3},{5,4},{6,5},{7,6},{9,8},{10,9},{11,10},{12... | collective-permute-start | bytes 98312 | tf_op jit(solution)/shard_map/ppermute | solution.py:20
  101.6 6.4 %collective-permute-start.2 = (f32[256,32]{0,1:T(8,128)S(1)}, f32[256,32]{0,1:T(8,128)S(1)}, u32[]{:S(2)}, u32[]{:S(2)}) collective-permute-start(f32[256,32]{0,1:T(8,128)S(1)} %get-tuple-element.18), channel_id=1, source_target_pairs={{0,1},{1,2},{2,3},{3,4},{4,5},{5,6},{6,7},{8,9},{9,10},{10,11},{11... | collective-permute-start | bytes 98312 | tf_op jit(solution)/shard_map/ppermute | solution.py:18
  206.4 7.0 %collective-permute-start.5 = (f32[256,32]{0,1:T(8,128)S(1)}, f32[256,32]{0,1:T(8,128)S(1)}, u32[]{:S(2)}, u32[]{:S(2)}) collective-permute-start(f32[256,32]{0,1:T(8,128)S(1)} %get-tuple-element.20), channel_id=1, source_target_pairs={{1,0},{2,1},{3,2},{4,3},{5,4},{6,5},{7,6},{9,8},{10,9},{11,10},{12... | collective-permute-start | bytes 98312 | tf_op jit(solution)/shard_map/ppermute | solution.py:20
  207.7 6.4 %collective-permute-start.4 = (f32[256,32]{0,1:T(8,128)S(1)}, f32[256,32]{0,1:T(8,128)S(1)}, u32[]{:S(2)}, u32[]{:S(2)}) collective-permute-start(f32[256,32]{0,1:T(8,128)S(1)} %get-tuple-element.20), channel_id=1, source_target_pairs={{0,1},{1,2},{2,3},{3,4},{4,5},{5,6},{6,7},{8,9},{9,10},{10,11},{11... | collective-permute-start | bytes 98312 | tf_op jit(solution)/shard_map/ppermute | solution.py:18
Sparse Core Ops, SparseCore 0:
  38.3 48.3 all-gather.4
where the time goes:
time: 323 us; the launch traced here: 321 us
  blocking collectives  219 us (68%)
  other arithmetic  27.5 us (9%)
  waiting for transfers between devices  24 us (7%)
  starting transfers between devices  19.2 us (6%)
  matrix products  15.9 us (5%)
  between operations  14.4 us (4%)
    psum x2, blocking collectives, local(): projected = lax.psum(local_gram(current, image), ('loop', 'inner'))  83.1 us
    psum x2, blocking collectives, local(): gram_total = lax.psum(local_gram(image, image), ('loop', 'inner'))  79.3 us
    psum x1, blocking collectives, local(): lax.psum(local_gram(start_block, start_block), ('loop', 'inner'))  42.3 us
    ppermute x3, starting transfers between devices, extended(): lax.ppermute(tail, axis, [(i, (i + 1) % count) for i in range(ends)])  15.1 us
    all_gather x2, blocking collectives, local(): vec_strip = lax.all_gather(vec_side[None], 'loop', axis=0, tiled=True)  14.3 us
    ppermute x3, waiting for transfers between devices, extended(): lax.ppermute(tail, axis, [(i, (i + 1) % count) for i in range(ends)])  13.8 us
    another operation x9, other arithmetic, finish(): lower_factor = jnp.linalg.cholesky(gram_total)  10.8 us
    ppermute x3, waiting for transfers between devices, extended(): lax.ppermute(head, axis, [((i + 1) % count, i) for i in range(ends)])  10.2 us
  transfers between devices with their start and end apart: 7, of which 4 were waited for; matrix products, arithmetic and copies ran while one was open for 3% of the time, Pallas kernels for 0%

commit v1 on v0

--- a/solution.py
+++ b/solution.py
@@ -2,6 +2,7 @@
 import jax.numpy as jnp
 from jax import lax
 from jax.sharding import PartitionSpec as P
+from jax.lax import psum
 
 STEPS = 2
 BINS_COL = 8
@@ -109,7 +110,9 @@
         image = image - jnp.dot(current, projected, precision=lax.Precision.HIGHEST)
         if lanczos_step > 0:
             image = image - jnp.dot(previous, prev_b.T, precision=lax.Precision.HIGHEST)
-        gram_total = lax.psum(local_gram(image, image), ("loop", "inner"))
+        gram_total = local_gram(image, image)
+        for no in ("inner", "loop"):
+            gram_total = psum(gram_total, axis_name=no)
         following, factor = finish(image, gram_total)
         coefficients.append(projected)
         coefficients.append(factor)

time: 323 us -> 332 us (1.028)
  blocking collectives: 219 us -> 229 us
    psum x2 -> x4, blocking collectives: 79.3 us -> 92.4 us  [local(): gram_total = psum(gram_total, axis_name=no)]
where the time goes in v1:
time: 332 us; the launch traced here: 331 us
  blocking collectives  229 us (69%)
  other arithmetic  27.5 us (8%)
  waiting for transfers between devices  23.9 us (7%)
  starting transfers between devices  18.9 us (6%)
  matrix products  15.9 us (5%)
  between operations  14.4 us (4%)
    psum x4, blocking collectives, local(): gram_total = psum(gram_total, axis_name=no)  92.4 us
    psum x2, blocking collectives, local(): projected = lax.psum(local_gram(current, image), ('loop', 'inner'))  80.9 us
    psum x1, blocking collectives, local(): lax.psum(local_gram(start_block, start_block), ('loop', 'inner'))  42.3 us
    ppermute x3, starting transfers between devices, extended(): lax.ppermute(tail, axis, [(i, (i + 1) % count) for i in range(ends)])  14.9 us
    ppermute x3, waiting for transfers between devices, extended(): lax.ppermute(tail, axis, [(i, (i + 1) % count) for i in range(ends)])  13.8 us
    all_gather x2, blocking collectives, local(): vec_strip = lax.all_gather(vec_side[None], 'loop', axis=0, tiled=True)  13.5 us
    another operation x9, other arithmetic, finish(): lower_factor = jnp.linalg.cholesky(gram_total)  10.8 us
    ppermute x3, waiting for transfers between devices, extended(): lax.ppermute(head, axis, [((i + 1) % count, i) for i in range(ends)])  10.2 us
  transfers between devices with their start and end apart: 7, of which 4 were waited for; matrix products, arithmetic and copies ran while one was open for 3% of the time, Pallas kernels for 0%

profile of v1, /device:TPU:0, one launch (start us, length us, event | category | flops | bytes accessed | tf_op | source)
XLA Modules:
  0.0 331.2 jit_solution(6104345148274427128)
XLA Ops:
  7.3 1.4 collective-permute-start.1
  8.7 5.5 %collective-permute-start = (bf16[256,1024]{1,0:T(8,128)(2,1)}, bf16[256,1024]{1,0:T(8,128)(2,1)S(1)}, u32[]{:S(2)}, u32[]{:S(2)}) collective-permute-start(bf16[256,1024]{1,0:T(8,128)(2,1)} %param.7), channel_id=1, source_target_pairs={{0,1},{1,2},{2,3},{3,4},{4,5},{5,6},{6,7},{8,9},{9,10},{10,11},{11... | collective-permute-start | bytes 1572872 | tf_op jit(solution)/shard_map/ppermute | solution.py:19
  14.2 10.2 %collective-permute-done.1 = bf16[256,1024]{1,0:T(8,128)(2,1)S(1)} collective-permute-done((bf16[256,1024]{1,0:T(8,128)(2,1)}, bf16[256,1024]{1,0:T(8,128)(2,1)S(1)}, u32[]{:S(2)}, u32[]{:S(2)}) %collective-permute-start.1) | collective-permute-done | bytes 524320 | tf_op jit(solution)/shard_map/ppermute | solution.py:21
  24.4 11.5 %collective-permute-done = bf16[256,1024]{1,0:T(8,128)(2,1)S(1)} collective-permute-done((bf16[256,1024]{1,0:T(8,128)(2,1)}, bf16[256,1024]{1,0:T(8,128)(2,1)S(1)}, u32[]{:S(2)}, u32[]{:S(2)}) %collective-permute-start) | collective-permute-done | bytes 524320 | tf_op jit(solution)/shard_map/ppermute | solution.py:19
  35.9 2.3 pad_maximum_fusion
  38.4 0.2 fusion.55
  38.6 0.2 fusion.56
  38.8 42.3 %psum.49 = f32[32,32]{0,1:T(8,128)S(1)} all-reduce(f32[32,32]{0,1:T(8,128)S(1)} %fusion.56), channel_id=1, replica_groups=mesh['loop'=4,'inner'=8] {'loop','inner'}, use_global_device_ids=true, to_apply=%region_0.1 | all-reduce | flops 1024 | bytes 8192 | tf_op jit(solution)/shard_map/psum | solution.py:96
  81.2 2.9 cholesky.59
  84.1 0.6 compare_reduce_fusion.2
  84.8 0.7 fusion.35
  85.4 2.4 custom-call.7
  88.1 0.3 fusion.20
  88.4 0.3 fusion.9
  88.7 4.2 %multiply_reduce_fusion = f32[3072]{0:T(1024)S(1)} fusion(bf16[3072,1024]{1,0:T(8,128)(2,1)} %all-gather.5.cloned.1.call-done), kind=kLoop, calls=%fused_computation | loop fusion | flops 9434112 | bytes 6303744 | tf_op jit(solution)/shard_map/reduce_sum | solution.py:83
  92.9 0.4 copy-done.1
  93.3 4.0 %fusion.4 = f32[256,3072]{1,0:T(8,128)} fusion(bf16[3072,1024]{1,0:T(8,128)(2,1)S(1)} %copy-done.1, bf16[256,1024]{1,0:T(8,128)(2,1)S(1)} %copy-done.2, f32[3072]{0:T(1024)S(1)} %multiply_reduce_fusion, f32[256]{0:T(256)S(1)} %multiply_reduce_fusion.1), kind=kOutput, calls=%fused_computation.7 | convolution fusion | flops 1614544896 | bytes 9974784 | tf_op jit(solution)/shard_map/dot_general | solution.py:84
  97.3 2.8 fusion.52
  100.1 0.2 broadcast_multiply_fusion.1
  100.3 1.3 collective-permute-start.3
  101.6 4.8 %collective-permute-start.2 = (f32[256,32]{0,1:T(8,128)S(1)}, f32[256,32]{0,1:T(8,128)S(1)}, u32[]{:S(2)}, u32[]{:S(2)}) collective-permute-start(f32[256,32]{0,1:T(8,128)S(1)} %get-tuple-element.18), channel_id=1, source_target_pairs={{0,1},{1,2},{2,3},{3,4},{4,5},{5,6},{6,7},{8,9},{9,10},{10,11},{11... | collective-permute-start | bytes 98312 | tf_op jit(solution)/shard_map/ppermute | solution.py:19
  106.4 1.6 collective-permute-done.2
  108.0 7.2 %all-gather.1 = f32[3072,32]{0,1:T(8,128)S(1)} all-gather(f32[768,32]{0,1:T(8,128)S(1)} %pad_maximum_fusion.1), channel_id=3, replica_groups=mesh['loop'=4,'inner'=8] {'loop'}, dimensions={0}, use_global_device_ids=true | all-gather | bytes 491520 | tf_op jit(solution)/shard_map/all_gather | solution.py:105
  115.2 2.8 convolution_multiply_fusion.3
  118.1 41.4 %psum.50 = f32[32,32]{0,1:T(8,128)S(1)} all-reduce(f32[32,32]{0,1:T(8,128)S(1)} %fusion.57), channel_id=1, replica_groups=mesh['loop'=4,'inner'=8] {'loop','inner'}, use_global_device_ids=true, to_apply=%region_6.9 | all-reduce | flops 1024 | bytes 8192 | tf_op jit(solution)/shard_map/psum | solution.py:109
  159.9 36.1 %psum.51 = f32[32,32]{0,1:T(8,128)S(1)} all-reduce(f32[32,32]{0,1:T(8,128)S(1)} %fusion.58), channel_id=1, replica_groups=mesh['loop'=4,'inner'=8] {'inner'}, use_global_device_ids=true, to_apply=%region_7.10 | all-reduce | flops 1024 | bytes 8192 | tf_op jit(solution)/shard_map/psum | solution.py:115
  196.0 10.1 %psum.52 = f32[32,32]{0,1:T(8,128)S(1)} all-reduce(f32[32,32]{0,1:T(8,128)S(1)} %psum.51), channel_id=1, replica_groups=mesh['loop'=4,'inner'=8] {'loop'}, use_global_device_ids=true, to_apply=%region_8.11 | all-reduce | flops 1024 | bytes 8192 | tf_op jit(solution)/shard_map/psum | solution.py:115
  206.2 2.9 cholesky.70
  209.1 0.6 compare_reduce_fusion.1
  209.8 0.7 fusion.43
  210.4 2.4 custom-call.8
  212.9 0.2 broadcast_multiply_fusion
  213.1 1.3 collective-permute-start.5
  214.4 4.5 %collective-permute-start.4 = (f32[256,32]{0,1:T(8,128)S(1)}, f32[256,32]{0,1:T(8,128)S(1)}, u32[]{:S(2)}, u32[]{:S(2)}) collective-permute-start(f32[256,32]{0,1:T(8,128)S(1)} %get-tuple-element.20), channel_id=1, source_target_pairs={{0,1},{1,2},{2,3},{3,4},{4,5},{5,6},{6,7},{8,9},{9,10},{10,11},{11... | collective-permute-start | bytes 98312 | tf_op jit(solution)/shard_map/ppermute | solution.py:19
  219.0 0.9 fusion.44
  219.9 0.7 collective-permute-done.4
  220.6 6.3 %all-gather.2 = f32[3072,32]{0,1:T(8,128)S(1)} all-gather(f32[768,32]{0,1:T(8,128)S(1)} %pad_maximum_fusion.2), channel_id=4, replica_groups=mesh['loop'=4,'inner'=8] {'loop'}, dimensions={0}, use_global_device_ids=true | all-gather | bytes 491520 | tf_op jit(solution)/shard_map/all_gather | solution.py:105
  226.9 2.8 convolution_multiply_fusion.2
  229.8 39.5 %psum.53 = f32[32,32]{0,1:T(8,128)S(1)} all-reduce(f32[32,32]{0,1:T(8,128)S(1)} %fusion.59), channel_id=1, replica_groups=mesh['loop'=4,'inner'=8] {'loop','inner'}, use_global_device_ids=true, to_apply=%region_9.12 | all-reduce | flops 1024 | bytes 8192 | tf_op jit(solution)/shard_map/psum | solution.py:109
  269.7 36.1 %psum.54 = f32[32,32]{0,1:T(8,128)S(1)} all-reduce(f32[32,32]{0,1:T(8,128)S(1)} %fusion.60), channel_id=1, replica_groups=mesh['loop'=4,'inner'=8] {'inner'}, use_global_device_ids=true, to_apply=%region_10.13 | all-reduce | flops 1024 | bytes 8192 | tf_op jit(solution)/shard_map/psum | solution.py:115
  305.8 10.1 %psum.55 = f32[32,32]{0,1:T(8,128)S(1)} all-reduce(f32[32,32]{0,1:T(8,128)S(1)} %psum.54), channel_id=1, replica_groups=mesh['loop'=4,'inner'=8] {'loop'}, use_global_device_ids=true, to_apply=%region_11.14 | all-reduce | flops 1024 | bytes 8192 | tf_op jit(solution)/shard_map/psum | solution.py:115
  316.0 2.9 cholesky.81
  319.0 0.6 compare_reduce_fusion
  319.6 0.7 fusion.42
  320.3 2.4 custom-call.9
  322.7 0.2 convolution_bitcast_fusion
  323.0 0.6 pad_maximum_fusion.3
  323.6 0.7 copy.35
  (42 shorter events, 1.8 us)
Async XLA Ops:
  7.2 31.2 %copy-start = (bf16[1024,32]{0,1:T(8,128)(2,1)S(1)}, bf16[1024,32]{0,1:T(8,128)(2,1)}, u32[]{:S(2)}) copy-start(bf16[1024,32]{0,1:T(8,128)(2,1)} %param.10) | copy-start | bytes 196612
  7.2 31.2 %copy-start.2 = (bf16[256,1024]{1,0:T(8,128)(2,1)S(1)}, bf16[256,1024]{1,0:T(8,128)(2,1)}, u32[]{:S(2)}) copy-start(bf16[256,1024]{1,0:T(8,128)(2,1)} %param.7) | copy-start | bytes 1572868
  7.2 31.0 %copy-start.3 = (s32[8192]{0:T(1024)S(1)}, s32[8192]{0:T(1024)}, u32[]{:S(2)}) copy-start(s32[8192]{0:T(1024)} %param.8) | copy-start | bytes 98308
  7.2 80.9 %copy-start.4 = (s32[256,2]{0,1:T(2,128)S(1)}, s32[256,2]{0,1:T(2,128)}, u32[]{:S(2)}) copy-start(s32[256,2]{0,1:T(2,128)} %param.9) | copy-start | bytes 6148
  7.2 81.4 %all-gather.5.cloned.1.call-start = ((), (), s32[]{:S(2)}) async-start(), calls=%async_computation | async-start | bytes 7864320 | tf_op jit(solution)/shard_map/all_gather | solution.py:55
  7.3 17.1 %collective-permute-start.1 = (bf16[256,1024]{1,0:T(8,128)(2,1)}, bf16[256,1024]{1,0:T(8,128)(2,1)S(1)}, u32[]{:S(2)}, u32[]{:S(2)}) collective-permute-start(bf16[256,1024]{1,0:T(8,128)(2,1)} %param.7), channel_id=1, source_target_pairs={{1,0},{2,1},{3,2},{4,3},{5,4},{6,5},{7,6},{9,8},{10,9},{11,10},{12... | collective-permute-start | bytes 1572872 | tf_op jit(solution)/shard_map/ppermute | solution.py:21
  8.7 27.2 %collective-permute-start = (bf16[256,1024]{1,0:T(8,128)(2,1)}, bf16[256,1024]{1,0:T(8,128)(2,1)S(1)}, u32[]{:S(2)}, u32[]{:S(2)}) collective-permute-start(bf16[256,1024]{1,0:T(8,128)(2,1)} %param.7), channel_id=1, source_target_pairs={{0,1},{1,2},{2,3},{3,4},{4,5},{5,6},{6,7},{8,9},{9,10},{10,11},{11... | collective-permute-start | bytes 1572872 | tf_op jit(solution)/shard_map/ppermute | solution.py:19
  88.7 4.6 %copy-start.1 = (bf16[3072,1024]{1,0:T(8,128)(2,1)S(1)}, bf16[3072,1024]{1,0:T(8,128)(2,1)}, u32[]{:S(2)}) copy-start(bf16[3072,1024]{1,0:T(8,128)(2,1)} %all-gather.5.cloned.1.call-done) | copy-start | bytes 18874372
  100.3 6.1 %collective-permute-start.3 = (f32[256,32]{0,1:T(8,128)S(1)}, f32[256,32]{0,1:T(8,128)S(1)}, u32[]{:S(2)}, u32[]{:S(2)}) collective-permute-start(f32[256,32]{0,1:T(8,128)S(1)} %get-tuple-element.18), channel_id=1, source_target_pairs={{1,0},{2,1},{3,2},{4,3},{5,4},{6,5},{7,6},{9,8},{10,9},{11,10},{12... | collective-permute-start | bytes 98312 | tf_op jit(solution)/shard_map/ppermute | solution.py:21
  101.6 6.4 %collective-permute-start.2 = (f32[256,32]{0,1:T(8,128)S(1)}, f32[256,32]{0,1:T(8,128)S(1)}, u32[]{:S(2)}, u32[]{:S(2)}) collective-permute-start(f32[256,32]{0,1:T(8,128)S(1)} %get-tuple-element.18), channel_id=1, source_target_pairs={{0,1},{1,2},{2,3},{3,4},{4,5},{5,6},{6,7},{8,9},{9,10},{10,11},{11... | collective-permute-start | bytes 98312 | tf_op jit(solution)/shard_map/ppermute | solution.py:19
  213.1 6.7 %collective-permute-start.5 = (f32[256,32]{0,1:T(8,128)S(1)}, f32[256,32]{0,1:T(8,128)S(1)}, u32[]{:S(2)}, u32[]{:S(2)}) collective-permute-start(f32[256,32]{0,1:T(8,128)S(1)} %get-tuple-element.20), channel_id=1, source_target_pairs={{1,0},{2,1},{3,2},{4,3},{5,4},{6,5},{7,6},{9,8},{10,9},{11,10},{12... | collective-permute-start | bytes 98312 | tf_op jit(solution)/shard_map/ppermute | solution.py:21
  214.4 6.1 %collective-permute-start.4 = (f32[256,32]{0,1:T(8,128)S(1)}, f32[256,32]{0,1:T(8,128)S(1)}, u32[]{:S(2)}, u32[]{:S(2)}) collective-permute-start(f32[256,32]{0,1:T(8,128)S(1)} %get-tuple-element.20), channel_id=1, source_target_pairs={{0,1},{1,2},{2,3},{3,4},{4,5},{5,6},{6,7},{8,9},{9,10},{10,11},{11... | collective-permute-start | bytes 98312 | tf_op jit(solution)/shard_map/ppermute | solution.py:19
Sparse Core Ops, SparseCore 0:
  38.3 48.3 all-gather.4
